TPU v7x, 32 devices: a whole 2x2x4 slice. The times are simulated.
32 devices in a mesh: tile: 4 (over y, core), tm: 8 (over z, x).
Axes of the slice: x: 2, y: 2, z: 4, core: 2. Of those that a mesh axis runs over, the one named last changes fastest.
Arguments:
- pixels: bfloat16 [192, 16, 64, 256], P(('tile', 'tm')), may hold values from -6 to 6
- slot_tile: int32 [192], replicated, may hold values from -1 to 95, as said below
- w_space: bfloat16 [3, 3, 256, 512], replicated, may hold values from -0.125 to 0.125
- b_space: float32 [512], replicated, may hold values from -3 to 3
- w_time: bfloat16 [3, 512, 512], replicated, may hold values from -0.15625 to 0.15625
- b_time: float32 [512], replicated, may hold values from -3 to 3
- gain: float32 [512], replicated, may hold values from 0.1 to 1.9
Outputs:
- latent: bfloat16 [96, 16, 16, 512], P('tile', 'tm')
Inputs may be any that keep to these rules, and one draw needn't show every extreme that they name: `slot_tile`: every tile id 0..95 stands in exactly one slot, -1 marks an empty slot. On each device (the 6 slots of one device in order) the live slots come first; the devices form aligned blocks of four consecutive devices whose live slots number 2 * 3, 3, 3 and 0 in some order. A group is 24 consecutive tile ids (tile id // 24); at most 2 slots of one device hold tiles of one group, and some device holds exactly 2 of one group.
All inputs are finite; a program needn't handle non-finite values.
Results may differ from a plain program's by a relative error of at most 0.0044.
Values may be sent and summed in bfloat16 or wider, within the bound.
A program may use at most 64 MiB of HBM per device.

v0:
```python
import jax
import jax.numpy as jnp
from jax import lax
from jax.sharding import PartitionSpec as P

TILE_SIDE = 8


def from_behind(value, axis, by):
    count = lax.axis_size(axis)
    pairs = [(i, i + by) for i in range(count) if 0 <= i + by < count]
    return lax.ppermute(value, axis, pairs)


def conv_space(raw_tiles, w_space, b_space):
    number, frames, pix_count, channels = raw_tiles.shape
    grid = raw_tiles.reshape(number * frames, TILE_SIDE, TILE_SIDE, channels)
    total = lax.conv_general_dilated(
        grid,
        w_space,
        (2, 2),
        ((1, 1), (1, 1)),
        dimension_numbers=("NHWC", "HWIO", "NHWC"),
        preferred_element_type=jnp.float32,
    )
    active = jax.nn.silu(total + b_space)
    half_side = TILE_SIDE // 2
    return active.astype(jnp.bfloat16).reshape(number, frames, half_side * half_side, -1)


def mix_time(extended, w_time, b_time, gain):
    number, all_frames, positions, channels = extended.shape
    frames = all_frames - 2
    total = jnp.zeros((number * frames * positions, channels), jnp.float32) + b_time
    for lag in range(3):
        segment = extended[:, 2 - lag : 2 - lag + frames].reshape(-1, channels)
        total = total + jnp.dot(segment, w_time[lag], preferred_element_type=jnp.float32)
    mixed = extended[:, 2:].reshape(-1, channels).astype(jnp.float32) + total
    scale = lax.rsqrt(jnp.mean(mixed * mixed, axis=-1, keepdims=True) + 1e-06)
    return (mixed * scale * gain).astype(jnp.bfloat16).reshape(number, frames, positions, channels)


def bucket_table(slot_tile, device_count, capacity, group_count, per_group, group_tiles):
    table = slot_tile.reshape(device_count, capacity)
    is_live = table >= 0
    group_of = jnp.where(is_live, table // group_tiles, group_count)
    slot_pos = jnp.arange(capacity, dtype=jnp.int32)
    earlier = slot_pos[None, :] < slot_pos[:, None]
    same_group = (group_of[:, :, None] == group_of[:, None, :]) & earlier[None, :, :]
    rank_of = jnp.sum(same_group.astype(jnp.int32), axis=2)
    target_slot = jnp.where(is_live, group_of * per_group + rank_of, -1)
    bucket_pos = jnp.arange(group_count * per_group, dtype=jnp.int32)
    matches = target_slot[:, None, :] == bucket_pos[None, :, None]
    sources = jnp.sum(jnp.where(matches, slot_pos[None, None, :], 0), axis=2)
    tile_at = jnp.sum(jnp.where(matches, table[:, None, :] + 1, 0), axis=2) - 1
    return (sources, tile_at)


def body(pixels, slot_tile, w_space, b_space, w_time, b_time, gain):
    tile_count = lax.axis_size("tile")
    slab_count = lax.axis_size("tm")
    capacity = pixels.shape[0]
    device_count = slot_tile.shape[0] // capacity
    group_tiles = capacity // 2 * slab_count
    per_group = (capacity + tile_count - 1) // tile_count
    my_group = lax.axis_index("tile")
    my_device = my_group * slab_count + lax.axis_index("tm")
    sources, tile_at = bucket_table(
        slot_tile, device_count, capacity, tile_count, per_group, group_tiles
    )
    own_sources = jnp.take(sources, my_device, axis=0)
    arrived = tile_at.reshape(tile_count, slab_count, tile_count, per_group)
    arrived = jnp.take(arrived, my_group, axis=2)
    arrived = jnp.transpose(arrived, (1, 0, 2)).reshape(-1)
    wanted = my_group * group_tiles + jnp.arange(group_tiles, dtype=jnp.int32)
    received_pos = jnp.arange(arrived.shape[0], dtype=jnp.int32)
    picked = jnp.sum(
        jnp.where(arrived[None, :] == wanted[:, None], received_pos[None, :], 0), axis=1
    )
    spatial = conv_space(pixels, w_space, b_space)
    outgoing = jnp.take(spatial, own_sources, axis=0)
    incoming = lax.all_to_all(
        lax.all_to_all(outgoing, "tile", split_axis=0, concat_axis=0, tiled=True),
        "tm",
        split_axis=1,
        concat_axis=0,
        tiled=True,
    )
    slab_feats = jnp.take(incoming, picked, axis=0)
    slab_len = slab_feats.shape[1]
    before = from_behind(slab_feats, "tm", 1)
    extended = jnp.concatenate([before, slab_feats], axis=1)
    return mix_time(extended, w_time, b_time, gain)


def solution(mesh):
    return jax.shard_map(
        body,
        mesh=mesh,
        in_specs=(P(("tile", "tm"), None, None, None), P(), P(), P(), P(), P(), P()),
        out_specs=P("tile", "tm", None, None),
        check_vma=False,
    )
```

profile of v0, /device:TPU:24, one launch (start us, length us, event | category | flops | bytes accessed | tf_op | source)
XLA Modules:
  0.0 132.7 jit_solution(15101436834196429223)
XLA Ops:
  0.0 0.0 copy-start
  0.0 0.8 compare_and_fusion.2
  0.8 0.7 broadcast_divide_fusion
  1.5 0.1 ge.45
  1.7 0.1 copy.41
  1.8 0.1 div.31
  1.9 0.1 copy.37
  1.9 0.1 and.52
  2.1 0.1 copy.38
  2.2 0.1 convert_reduce_fusion
  2.3 0.1 add.128
  2.4 0.1 copy.42
  2.5 0.2 select_reduce_fusion.3
  2.7 0.0 copy-done
  2.7 6.6 %multiply_convert_fusion = bf16[96,4,4,512]{3,0,2,1:T(8,128)(2,1)S(1)} fusion(bf16[3,3,256,512]{3,2,1,0:T(8,128)(2,1)S(1)} %copy-done, bf16[96,8,8,256]{3,2,1,0:T(8,128)(2,1)} %bitcast.48, f32[512]{0:T(512)} %param.10), kind=kOutput, calls=%fused_computation.4 | convolution fusion | flops 3049783296 | bytes 7079936 | tf_op jit(solution)/shard_map/conv_general_dilated | solution.py:18
  9.3 2.0 %copy.45 = bf16[6,16,16,512]{3,2,1,0:T(8,128)(2,1)} copy(bf16[6,16,16,512]{3,1,0,2:T(8,128)(2,1)S(1)} %bitcast.47) | data formatting | bytes 3145728 | tf_op jit(solution)/shard_map/reshape | solution.py:28
  11.4 3.4 %gather_fusion = bf16[8,16,16,512]{3,2,1,0:T(8,128)(2,1)} fusion(bf16[6,16,16,512]{3,2,1,0:T(8,128)(2,1)} %copy.45, s32[1024]{0:T(1024)S(1)} %pad_clamp_fusion.1), kind=kCustom, calls=%fused_computation | custom fusion | bytes 4194336 | tf_op jit(solution)/shard_map/jit(_take)/gather | solution.py:81
  14.8 1.9 %broadcast_select_fusion = bf16[8,16,16,512]{3,2,1,0:T(8,128)(2,1)S(1)} fusion(bf16[8,16,16,512]{3,2,1,0:T(8,128)(2,1)} %gather_fusion, pred[8]{0:T(512)(128)(4,1)S(1)} %compare_and_fusion), kind=kLoop, calls=%fused_computation.5 | loop fusion | flops 1048576 | bytes 4194312 | tf_op jit(solution)/shard_map/jit(_take)/select_n | solution.py:81
  16.7 28.3 %all_to_all.23 = bf16[8,16,16,512]{3,2,1,0:T(8,128)(2,1)S(1)} all-to-all(bf16[8,16,16,512]{3,2,1,0:T(8,128)(2,1)S(1)} %broadcast_select_fusion), channel_id=1, replica_groups=mesh['tile'=4,'tm'=8] {'tile'}, dimensions={0} | all-to-all | bytes 4194304 | tf_op jit(solution)/shard_map/all_to_all | solution.py:83
  44.9 1.5 %copy.46 = bf16[8,16,16,512]{3,2,0,1:T(8,128)(2,1)} copy(bf16[8,16,16,512]{3,2,1,0:T(8,128)(2,1)S(1)} %all_to_all.23) | data formatting | bytes 4194304 | tf_op jit(solution)/shard_map/all_to_all | solution.py:83
  46.4 6.0 %all-to-all-start.1 = ((bf16[8,16,16,512]{3,2,0,1:T(8,128)(2,1)}), bf16[8,16,16,512]{3,2,0,1:T(8,128)(2,1)}, u32[]{:S(2)}, u32[]{:S(2)}) async-start(bf16[8,16,16,512]{3,2,0,1:T(8,128)(2,1)} %copy.46), calls=%async_computation.1 | async-start | bytes 4194304 | tf_op jit(solution)/shard_map/all_to_all | solution.py:82
  52.5 0.1 sub.14
  52.5 0.1 copy.43
  52.7 0.1 eq.47
  52.8 0.2 select_reduce_fusion.2
  53.0 45.9 %all-to-all-done.1 = bf16[8,16,16,512]{3,2,0,1:T(8,128)(2,1)} async-done(((bf16[8,16,16,512]{3,2,0,1:T(8,128)(2,1)}), bf16[8,16,16,512]{3,2,0,1:T(8,128)(2,1)}, u32[]{:S(2)}, u32[]{:S(2)}) %all-to-all-start.1) | async-done | bytes 2097184 | tf_op jit(solution)/shard_map/all_to_all | solution.py:82
  98.9 3.1 %copy.48 = bf16[8,8,2,16,512]{4,3,2,1,0:T(8,128)(2,1)} copy(bf16[8,8,2,16,512]{4,3,1,2,0:T(8,128)(2,1)} %bitcast.7) | data formatting | bytes 4194304 | tf_op jit(solution)/shard_map/all_to_all | solution.py:82
  102.0 2.2 %gather_fusion.1 = bf16[24,2,16,512]{3,2,1,0:T(8,128)(2,1)S(1)} fusion(bf16[64,2,16,512]{3,2,1,0:T(8,128)(2,1)} %bitcast.45, s32[1024]{0:T(1024)S(1)} %pad_clamp_fusion), kind=kCustom, calls=%fused_computation.1 | custom fusion | bytes 1572960 | tf_op jit(solution)/shard_map/jit(_take)/gather | solution.py:89
  104.2 1.0 broadcast_select_fusion.1
  105.2 2.5 %collective-permute-start = (bf16[24,2,16,512]{3,2,1,0:T(8,128)(2,1)}, bf16[24,2,16,512]{3,2,1,0:T(8,128)(2,1)}, u32[]{:S(2)}, u32[]{:S(2)}) collective-permute-start(bf16[24,2,16,512]{3,2,1,0:T(8,128)(2,1)} %broadcast_select_fusion.1), channel_id=1, source_target_pairs={{0,1},{1,2},{2,3},{3,4},{4,5},{5,6},{6,7},{8,9},{9,10},{10,11},{11... | collective-permute-start | bytes 2359304 | tf_op jit(solution)/shard_map/ppermute | solution.py:12
  107.8 0.1 broadcast_in_dim.109
  107.9 0.1 broadcast_in_dim.110
  108.0 0.0 copy-start.1
  108.0 2.0 %fusion.10 = f32[768,512]{1,0:T(8,128)S(1)} fusion(bf16[768,512]{1,0:T(8,128)(2,1)} %bitcast.12, bf16[3,512,512]{2,1,0:T(8,128)(2,1)} %param.11), kind=kOutput, calls=%fused_computation.16 | convolution fusion | flops 402653184 | bytes 2883584 | tf_op jit(solution)/shard_map/dot_general | solution.py:37
  110.0 0.0 copy-start.2
  110.0 17.8 %collective-permute-done = bf16[24,2,16,512]{3,2,1,0:T(8,128)(2,1)} collective-permute-done((bf16[24,2,16,512]{3,2,1,0:T(8,128)(2,1)}, bf16[24,2,16,512]{3,2,1,0:T(8,128)(2,1)}, u32[]{:S(2)}, u32[]{:S(2)}) %collective-permute-start) | collective-permute-done | bytes 786464 | tf_op jit(solution)/shard_map/ppermute | solution.py:12
  127.8 1.2 pad_maximum_fusion
  129.0 0.0 copy-done.1
  129.0 0.6 fusion.8
  129.6 0.0 copy-done.2
  129.6 0.0 copy-start.3
  129.6 2.0 %multiply_reduce_fusion = (f32[768]{0:T(1024)S(1)}, f32[768,512]{1,0:T(8,128)S(1)}) fusion(bf16[768,512]{1,0:T(8,128)(2,1)} %bitcast.16, bf16[3,512,512]{2,1,0:T(8,128)(2,1)S(1)} %copy-done.1, f32[768,512]{1,0:T(8,128)S(1)} %fusion.8, f32[768,512]{1,0:T(8,128)S(1)} %fusion.10, f32[512]{0:T(512)S(1)} %copy-done.2, ...), kind=kOutput, calls=%fused_computation.7 | convolution fusion | flops 405798144 | bytes 6821888 | tf_op jit(solution)/shard_map/dot_general | solution.py:37
  131.6 0.0 copy-done.3
  131.6 1.1 multiply_convert_fusion.1
  (14 shorter events, 0.1 us)
Async XLA Ops:
  0.0 2.7 %copy-start = (bf16[3,3,256,512]{3,2,1,0:T(8,128)(2,1)S(1)}, bf16[3,3,256,512]{3,2,1,0:T(8,128)(2,1)}, u32[]{:S(2)}) copy-start(bf16[3,3,256,512]{3,2,1,0:T(8,128)(2,1)} %param.9) | copy-start | bytes 7077892
  46.4 52.5 %all-to-all-start.1 = ((bf16[8,16,16,512]{3,2,0,1:T(8,128)(2,1)}), bf16[8,16,16,512]{3,2,0,1:T(8,128)(2,1)}, u32[]{:S(2)}, u32[]{:S(2)}) async-start(bf16[8,16,16,512]{3,2,0,1:T(8,128)(2,1)} %copy.46), calls=%async_computation.1 | async-start | bytes 4194304 | tf_op jit(solution)/shard_map/all_to_all | solution.py:82
  105.2 22.6 %collective-permute-start = (bf16[24,2,16,512]{3,2,1,0:T(8,128)(2,1)}, bf16[24,2,16,512]{3,2,1,0:T(8,128)(2,1)}, u32[]{:S(2)}, u32[]{:S(2)}) collective-permute-start(bf16[24,2,16,512]{3,2,1,0:T(8,128)(2,1)} %broadcast_select_fusion.1), channel_id=1, source_target_pairs={{0,1},{1,2},{2,3},{3,4},{4,5},{5,6},{6,7},{8,9},{9,10},{10,11},{11... | collective-permute-start | bytes 2359304 | tf_op jit(solution)/shard_map/ppermute | solution.py:12
  108.0 21.0 %copy-start.1 = (bf16[3,512,512]{2,1,0:T(8,128)(2,1)S(1)}, bf16[3,512,512]{2,1,0:T(8,128)(2,1)}, u32[]{:S(2)}) copy-start(bf16[3,512,512]{2,1,0:T(8,128)(2,1)} %param.11) | copy-start | bytes 4718596
  110.0 19.6 %copy-start.2 = (f32[512]{0:T(512)S(1)}, f32[512]{0:T(512)}, u32[]{:S(2)}) copy-start(f32[512]{0:T(512)} %param.12) | copy-start | bytes 6148
  129.6 2.1 %copy-start.3 = (f32[512]{0:T(512)S(1)}, f32[512]{0:T(512)}, u32[]{:S(2)}) copy-start(f32[512]{0:T(512)} %param.13) | copy-start | bytes 6148
where the time goes:
time: 133 us
  waiting for transfers between devices  63.7 us (48%)
  blocking collectives  28.3 us (21%)
  local copies, waits for them, and re-layouts  13.6 us (10%)
  matrix products  11.2 us (8%)
  starting transfers between devices  8.57 us (6%)
  other arithmetic  7.24 us (5%)
    all_to_all x1, waiting for transfers between devices, body(): lax.all_to_all(lax.all_to_all(outgoing, 'tile', split_axis=0, concat_axis...  45.9 us
    all_to_all x1, blocking collectives, body(): lax.all_to_all(outgoing, 'tile', split_axis=0, concat_axis=0, tiled=True)  28.3 us
    ppermute x1, waiting for transfers between devices, from_behind(): return lax.ppermute(value, axis, pairs)  17.8 us
    conv_general_dilated x1, matrix products, conv_space(): lax.conv_general_dilated(grid, w_space, (2, 2), ((1, 1), (1, 1)), dimensi...  6.59 us
    all_to_all x1, starting transfers between devices, body(): lax.all_to_all(lax.all_to_all(outgoing, 'tile', split_axis=0, concat_axis...  6.02 us
    dot_general x3, matrix products, mix_time(): jnp.dot(segment, w_time[lag], preferred_element_type=jnp.float32)  4.56 us
    gather x1, local copies, waits for them, and re-layouts, body(): outgoing = jnp.take(spatial, own_sources, axis=0)  3.44 us
    all_to_all x1, local copies, waits for them, and re-layouts, body(): lax.all_to_all(lax.all_to_all(outgoing, 'tile', split_axis=0, concat_axis...  3.13 us
  transfers between devices with their start and end apart: 2, of which 2 were waited for; matrix products, arithmetic and copies ran while one was open for 2% of the time, Pallas kernels for 0%

commit v1 on v0

v1 whole, which is shorter than its diff:
```python
import functools

import jax
import jax.numpy as jnp
from jax import lax
from jax.experimental import pallas as pl
from jax.experimental.pallas import tpu as pltpu
from jax.sharding import PartitionSpec as P

TILE_SIDE = 8


def conv_space(raw_tiles, w_space, b_space):
    number, frames, pix_count, channels = raw_tiles.shape
    grid = raw_tiles.reshape(number * frames, TILE_SIDE, TILE_SIDE, channels)
    total = lax.conv_general_dilated(
        grid,
        w_space,
        (2, 2),
        ((1, 1), (1, 1)),
        dimension_numbers=("NHWC", "HWIO", "NHWC"),
        preferred_element_type=jnp.float32,
    )
    active = jax.nn.silu(total + b_space)
    half_side = TILE_SIDE // 2
    return active.astype(jnp.bfloat16).reshape(number, frames, half_side * half_side, -1)


def tables(slot_tile, rows, groups, bucket, group_tiles, my_row):
    table = slot_tile.reshape(rows, -1)
    width = table.shape[1]
    group_of = jnp.where(table >= 0, lax.div(table, group_tiles), groups)
    pos = jnp.arange(width, dtype=jnp.int32)
    earlier = pos[None, :] < pos[:, None]
    same = (group_of[:, :, None] == group_of[:, None, :]) & earlier[None]
    rank = jnp.sum(same.astype(jnp.int32), axis=2)
    target = group_of * bucket + rank
    own_target = lax.dynamic_index_in_dim(target, my_row, 0, keepdims=False)
    own_live = lax.dynamic_index_in_dim(table, my_row, 0, keepdims=False) >= 0
    own_target = jnp.where(own_live, own_target, -1)
    places = jnp.arange(groups * bucket, dtype=jnp.int32)
    send_idx = jnp.sum(
        jnp.where(own_target[None, :] == places[:, None], pos[None, :], 0), axis=1
    )
    wanted = my_row * group_tiles + jnp.arange(group_tiles, dtype=jnp.int32)
    arrived = jnp.arange(rows, dtype=jnp.int32)[:, None] * bucket + rank
    pick_idx = jnp.sum(
        jnp.where(
            table.reshape(-1)[None, :] == wanted[:, None], arrived.reshape(-1)[None, :], 0
        ),
        axis=1,
    )
    return send_idx, pick_idx


def kernel(
    rows, slabs, cap, bucket, group_tiles,
    send_idx, pick_idx, src, w_time, b_time, gain, out,
    got1a, got1b, out2, got2a, got2b, feats, halo,
    send1, recv1, send2, recv2, send3, recv3,
):
    frames = 2
    got1, got2 = (got1a, got1b), (got2a, got2b)
    row = lax.axis_index("tile")
    slab = lax.axis_index("tm")
    barrier = pltpu.get_barrier_semaphore()
    for k in range(1, slabs):
        pl.semaphore_signal(barrier, inc=1, device_id={"tm": lax.rem(slab + k, slabs)})
    for k in range(1, rows):
        pl.semaphore_signal(barrier, inc=1, device_id={"tile": lax.rem(row + k, rows)})
    pl.semaphore_wait(barrier, slabs + rows - 2)

    def copy1(f, k):
        to = lax.rem(slab + k, slabs)
        return pltpu.make_async_remote_copy(
            src_ref=src.at[to, f],
            dst_ref=got1[f].at[pl.ds(slab * cap, cap)],
            send_sem=send1.at[f, k - 1],
            recv_sem=recv1.at[f, k - 1],
            device_id={"tm": to},
        )

    def copy2(f, k):
        to = lax.rem(row + k, rows)
        return pltpu.make_async_remote_copy(
            src_ref=out2.at[f, pl.ds(to * bucket, bucket)],
            dst_ref=got2[f].at[pl.ds(row * bucket, bucket)],
            send_sem=send2.at[f, k - 1],
            recv_sem=recv2.at[f, k - 1],
            device_id={"tile": to},
        )

    def copy3(f):
        return pltpu.make_async_remote_copy(
            src_ref=feats.at[f],
            dst_ref=halo.at[f],
            send_sem=send3.at[f],
            recv_sem=recv3.at[f],
            device_id={"tm": lax.rem(slab + 1, slabs)},
        )

    for f in range(frames):
        for k in range(1, slabs):
            copy1(f, k).start()
    for f in range(frames):
        got1[f][pl.ds(slab * cap, cap)] = src[slab, f]
        for k in range(1, slabs):
            copy1(f, k).wait_recv()

        @pl.loop(0, rows * bucket)
        def _(i):
            out2[f, i] = got1[f][send_idx[i]]

        for k in range(1, rows):
            copy2(f, k).start()

        @pl.loop(0, bucket)
        def _(j):
            got2[f][row * bucket + j] = got1[f][send_idx[row * bucket + j]]

        for k in range(1, rows):
            copy2(f, k).wait_recv()

        @pl.loop(0, group_tiles)
        def _(i):
            feats[f, i] = got2[f][pick_idx[i]]

        @pl.when(slab < slabs - 1)
        def _():
            copy3(f).start()

    for f in range(frames):

        @pl.when(slab > 0)
        def _():
            copy3(f).wait_recv()

        @pl.when(slab == 0)
        def _():
            halo[f] = jnp.zeros(halo.shape[1:], halo.dtype)

    part = group_tiles // 2

    @pl.loop(0, 2)
    def _(c):
        at = pl.ds(c * part, part)
        seq = [halo[0, at], halo[1, at], feats[0, at], feats[1, at]]
        seq = [v.reshape(part * 16, v.shape[-1]) for v in seq]
        for f in range(frames):
            mixed = seq[2 + f].astype(jnp.float32) + b_time[...]
            for lag in range(3):
                mixed = mixed + jnp.dot(
                    seq[2 + f - lag], w_time[lag], preferred_element_type=jnp.float32
                )
            scale = lax.rsqrt(jnp.mean(mixed * mixed, axis=-1, keepdims=True) + 1e-06)
            value = (mixed * scale * gain[...]).astype(jnp.bfloat16)
            out[at, f] = value.reshape(part, 16, value.shape[-1])

    for f in range(frames):
        for k in range(1, slabs):
            copy1(f, k).wait_send()
        for k in range(1, rows):
            copy2(f, k).wait_send()

        @pl.when(slab < slabs - 1)
        def _():
            copy3(f).wait_send()


def body(rows, slabs, pixels, slot_tile, w_space, b_space, w_time, b_time, gain):
    cap, all_frames = pixels.shape[:2]
    channels = w_space.shape[-1]
    group_tiles = cap // 2 * slabs
    per_group = (cap + rows - 1) // rows
    bucket = per_group * 3 * (slabs // 4)
    frames = all_frames // slabs
    send_idx, pick_idx = tables(
        slot_tile, rows, rows, bucket, group_tiles, lax.axis_index("tile")
    )
    spatial = conv_space(pixels, w_space, b_space)
    src = spatial.reshape(cap, slabs, frames, 16, channels).transpose(1, 2, 0, 3, 4)
    vmem = pl.BlockSpec(memory_space=pltpu.VMEM)
    smem = pl.BlockSpec(memory_space=pltpu.SMEM)
    bf16 = jnp.bfloat16
    dma = pltpu.SemaphoreType.DMA
    return pl.pallas_call(
        functools.partial(kernel, rows, slabs, cap, bucket, group_tiles),
        out_shape=jax.ShapeDtypeStruct((group_tiles, frames, 16, channels), bf16),
        in_specs=[smem, smem, vmem, vmem, vmem, vmem],
        out_specs=vmem,
        scratch_shapes=[
            pltpu.VMEM((slabs * cap, 16, channels), bf16),
            pltpu.VMEM((slabs * cap, 16, channels), bf16),
            pltpu.VMEM((frames, rows * bucket, 16, channels), bf16),
            pltpu.VMEM((rows * bucket, 16, channels), bf16),
            pltpu.VMEM((rows * bucket, 16, channels), bf16),
            pltpu.VMEM((frames, group_tiles, 16, channels), bf16),
            pltpu.VMEM((frames, group_tiles, 16, channels), bf16),
            dma((frames, slabs - 1)),
            dma((frames, slabs - 1)),
            dma((frames, rows - 1)),
            dma((frames, rows - 1)),
            dma((frames,)),
            dma((frames,)),
        ],
        compiler_params=pltpu.CompilerParams(collective_id=0, has_side_effects=True),
    )(send_idx, pick_idx, src, w_time, b_time[None], gain[None])


def solution(mesh):
    return jax.shard_map(
        functools.partial(body, mesh.shape["tile"], mesh.shape["tm"]),
        mesh=mesh,
        in_specs=(P(("tile", "tm"), None, None, None), P(), P(), P(), P(), P(), P()),
        out_specs=P("tile", "tm", None, None),
        check_vma=False,
    )
```

time: 133 us -> 85.1 us (0.64)
  the two profiles are of different devices: /device:TPU:24 before, /device:TPU:21 now
where the time goes in v1:
time: 85.1 us; the launch traced here: 84.8 us
  Pallas kernels  63.5 us (75%)
  local copies, waits for them, and re-layouts  10.2 us (12%)
  matrix products  8.75 us (10%)
  other arithmetic  2.3 us (3%)
    pallas_call x1, Pallas kernels, body(): pl.pallas_call(functools.partial(kernel, rows, slabs, cap, bucket, group_...  63.5 us
    conv_general_dilated x1, matrix products, conv_space(): lax.conv_general_dilated(grid, w_space, (2, 2), ((1, 1), (1, 1)), dimensi...  8.75 us
    another operation x2, local copies, waits for them, and re-layouts, body(): spatial.reshape(cap, slabs, frames, 16, channels).transpose(1, 2, 0, 3, 4)  7.08 us
    unnamed x3, local copies, waits for them, and re-layouts  2.09 us

profile of v1, /device:TPU:21, one launch (start us, length us, event | category | flops | bytes accessed | tf_op | source)
XLA Modules:
  0.0 84.8 jit_solution(13740281310042147177)
XLA Ops:
  0.0 0.0 copy-start
  0.0 0.9 %reshape.61 = s32[4,48]{1,0:T(4,128)S(1)} reshape(s32[192]{0:T(256)} %param.8) | data formatting | bytes 1536 | tf_op jit(solution)/shard_map/reshape | solution.py:30
  1.0 0.2 convert_reduce_fusion
  1.2 0.1 broadcast_add_fusion
  1.3 0.1 add.51
  1.3 1.3 %select_reduce_fusion.pick_idx = s32[24]{0:T(128)} fusion(s32[192]{0:T(256)S(1)} %add.51, s32[192]{0:T(256)} %param.8, s32[24]{0:T(128)S(1)} %iota_add_fusion), kind=kLoop, calls=%fused_computation.5 | loop fusion | flops 13800 | bytes 1728 | tf_op jit(solution)/shard_map/reduce_sum | solution.py:47
  2.7 0.6 select_reduce_fusion.1.send_idx
  3.3 0.0 copy-done
  3.3 8.7 %multiply_convert_fusion = bf16[96,4,4,512]{3,0,2,1:T(8,128)(2,1)} fusion(bf16[3,3,256,512]{3,2,1,0:T(8,128)(2,1)S(1)} %copy-done, bf16[96,8,8,256]{3,2,1,0:T(8,128)(2,1)} %bitcast.16, f32[512]{0:T(512)} %param.10), kind=kOutput, calls=%fused_computation.2 | convolution fusion | flops 3049783296 | bytes 7079936 | tf_op jit(solution)/shard_map/conv_general_dilated | solution.py:16
  12.1 3.6 %reshape.63 = bf16[6,8,2,16,512]{4,2,1,0,3:T(2,128)(2,1)} reshape(bf16[96,4,4,512]{3,0,2,1:T(8,128)(2,1)} %multiply_convert_fusion) | data formatting | bytes 3145728 | tf_op jit(solution)/shard_map/reshape;reshape | solution.py:181
  15.7 3.4 %copy.22 = bf16[6,8,2,16,512]{4,3,0,2,1:T(8,128)(2,1)} copy(bf16[6,8,2,16,512]{4,2,1,0,3:T(2,128)(2,1)} %reshape.63) | data formatting | bytes 3145728 | tf_op jit(solution)/shard_map/reshape;reshape | solution.py:181
  19.1 63.5 %shard_map.73 = bf16[24,2,16,512]{3,2,1,0:T(8,128)(2,1)} custom-call(s32[48]{0:T(128)} %select_reduce_fusion.1.send_idx, s32[24]{0:T(128)} %select_reduce_fusion.pick_idx, bf16[8,2,6,16,512]{4,3,2,1,0:T(8,128)(2,1)} %bitcast.13, bf16[3,512,512]{2,1,0:T(8,128)(2,1)} %w_time.1, f32[1,512]{1,0:T(1,128)} %bitcast.14, f32[1,512]{1,0:T(1,128)} %bitcast.15), custom_call_target="tpu_custom_call" | custom-call | tf_op jit(solution)/shard_map/pallas_call | solution.py:186
  82.7 2.1 %copy.24 = bf16[24,2,16,512]{3,2,1,0:T(8,128)(2,1)} copy(bf16[24,2,16,512]{3,2,1,0:T(8,128)(2,1)} %shard_map.73) | data formatting | bytes 1572864
  (5 shorter events, 0.0 us)
Async XLA Ops:
  0.0 3.3 %copy-start = (bf16[3,3,256,512]{3,2,1,0:T(8,128)(2,1)S(1)}, bf16[3,3,256,512]{3,2,1,0:T(8,128)(2,1)}, u32[]{:S(2)}) copy-start(bf16[3,3,256,512]{3,2,1,0:T(8,128)(2,1)} %param.9) | copy-start | bytes 7077892

commit v2 on v1

--- a/solution.py
+++ b/solution.py
@@ -73,7 +73,7 @@
     def copy1(f, k):
         to = lax.rem(slab + k, slabs)
         return pltpu.make_async_remote_copy(
-            src_ref=src.at[to, f],
+            src_ref=src.at[:, to * frames + f],
             dst_ref=got1[f].at[pl.ds(slab * cap, cap)],
             send_sem=send1.at[f, k - 1],
             recv_sem=recv1.at[f, k - 1],
@@ -103,7 +103,7 @@
         for k in range(1, slabs):
             copy1(f, k).start()
     for f in range(frames):
-        got1[f][pl.ds(slab * cap, cap)] = src[slab, f]
+        got1[f][pl.ds(slab * cap, cap)] = src[:, slab * frames + f]
         for k in range(1, slabs):
             copy1(f, k).wait_recv()
 
@@ -178,7 +178,6 @@
         slot_tile, rows, rows, bucket, group_tiles, lax.axis_index("tile")
     )
     spatial = conv_space(pixels, w_space, b_space)
-    src = spatial.reshape(cap, slabs, frames, 16, channels).transpose(1, 2, 0, 3, 4)
     vmem = pl.BlockSpec(memory_space=pltpu.VMEM)
     smem = pl.BlockSpec(memory_space=pltpu.SMEM)
     bf16 = jnp.bfloat16
@@ -204,7 +203,7 @@
             dma((frames,)),
         ],
         compiler_params=pltpu.CompilerParams(collective_id=0, has_side_effects=True),
-    )(send_idx, pick_idx, src, w_time, b_time[None], gain[None])
+    )(send_idx, pick_idx, spatial, w_time, b_time[None], gain[None])
 
 
 def solution(mesh):

time: 85.1 us -> 77.8 us (0.914)
  local copies, waits for them, and re-layouts: 10.2 us -> 5.14 us
  matrix products: 8.75 us -> 6.6 us
    another operation x2 -> x0, local copies, waits for them, and re-layouts: 7.08 us -> none  [body(): spatial.reshape(cap, slabs, frames, 16, channels).transpose(1, 2, 0, 3, 4)]
    conv_general_dilated x1, matrix products: 8.75 us -> 6.6 us  [conv_space(): lax.conv_general_dilated(grid, w_space, (2, 2), ((1, 1), (1, 1)), dimensi...]
    reshape x0 -> x1, local copies, waits for them, and re-layouts: none -> 2.05 us  [conv_space(): active.astype(jnp.bfloat16)]
where the time goes in v2:
time: 77.8 us; the launch traced here: 77.6 us
  Pallas kernels  63.5 us (82%)
  matrix products  6.6 us (8%)
  local copies, waits for them, and re-layouts  5.14 us (7%)
  other arithmetic  2.32 us (3%)
    pallas_call x1, Pallas kernels, body(): pl.pallas_call(functools.partial(kernel, rows, slabs, cap, bucket, group_...  63.5 us
    conv_general_dilated x1, matrix products, conv_space(): lax.conv_general_dilated(grid, w_space, (2, 2), ((1, 1), (1, 1)), dimensi...  6.6 us
    unnamed x3, local copies, waits for them, and re-layouts  2.09 us
    reshape x1, local copies, waits for them, and re-layouts, conv_space(): active.astype(jnp.bfloat16)  2.05 us

profile of v2, /device:TPU:21, one launch (start us, length us, event | category | flops | bytes accessed | tf_op | source)
XLA Modules:
  0.0 77.6 jit_solution(3790770294498681316)
XLA Ops:
  0.0 0.0 copy-start
  0.0 0.9 %reshape.64 = s32[4,48]{1,0:T(4,128)S(1)} reshape(s32[192]{0:T(256)} %param.8) | data formatting | bytes 1536 | tf_op jit(solution)/shard_map/reshape | solution.py:30
  1.0 0.2 convert_reduce_fusion
  1.2 0.1 broadcast_add_fusion
  1.3 0.1 add.51
  1.3 1.4 %select_reduce_fusion.pick_idx = s32[24]{0:T(128)} fusion(s32[192]{0:T(256)S(1)} %add.51, s32[192]{0:T(256)} %param.8, s32[24]{0:T(128)S(1)} %iota_add_fusion), kind=kLoop, calls=%fused_computation.4 | loop fusion | flops 13800 | bytes 1728 | tf_op jit(solution)/shard_map/reduce_sum | solution.py:47
  2.7 0.6 select_reduce_fusion.1.send_idx
  3.3 0.0 copy-done
  3.3 6.6 %multiply_convert_fusion = bf16[96,4,4,512]{3,0,2,1:T(8,128)(2,1)S(1)} fusion(bf16[3,3,256,512]{3,2,1,0:T(8,128)(2,1)S(1)} %copy-done, bf16[96,8,8,256]{3,2,1,0:T(8,128)(2,1)} %bitcast.10, f32[512]{0:T(512)} %param.10), kind=kOutput, calls=%fused_computation.2 | convolution fusion | flops 3049783296 | bytes 7079936 | tf_op jit(solution)/shard_map/conv_general_dilated | solution.py:16
  9.9 2.1 %copy.12.src = bf16[6,16,16,512]{3,2,1,0:T(8,128)(2,1)} copy(bf16[6,16,16,512]{3,1,0,2:T(8,128)(2,1)S(1)} %bitcast.7) | data formatting | bytes 3145728 | tf_op jit(solution)/shard_map/reshape | solution.py:26
  12.0 63.5 %shard_map.73 = bf16[24,2,16,512]{3,2,1,0:T(8,128)(2,1)} custom-call(s32[48]{0:T(128)} %select_reduce_fusion.1.send_idx, s32[24]{0:T(128)} %select_reduce_fusion.pick_idx, bf16[6,16,16,512]{3,2,1,0:T(8,128)(2,1)} %copy.12.src, bf16[3,512,512]{2,1,0:T(8,128)(2,1)} %w_time.1, f32[1,512]{1,0:T(1,128)} %bitcast.8, f32[1,512]{1,0:T(1,128)} %bitcast.9), custom_call_target="tpu_custom_call" | custom-call | tf_op jit(solution)/shard_map/pallas_call | solution.py:185
  75.5 2.1 %copy.18 = bf16[24,2,16,512]{3,2,1,0:T(8,128)(2,1)} copy(bf16[24,2,16,512]{3,2,1,0:T(8,128)(2,1)} %shard_map.73) | data formatting | bytes 1572864
  (5 shorter events, 0.0 us)
Async XLA Ops:
  0.0 3.3 %copy-start = (bf16[3,3,256,512]{3,2,1,0:T(8,128)(2,1)S(1)}, bf16[3,3,256,512]{3,2,1,0:T(8,128)(2,1)}, u32[]{:S(2)}) copy-start(bf16[3,3,256,512]{3,2,1,0:T(8,128)(2,1)} %param.9) | copy-start | bytes 7077892

commit v3 on v2

--- a/solution.py
+++ b/solution.py
@@ -56,7 +56,7 @@
 def kernel(
     rows, slabs, cap, bucket, group_tiles,
     send_idx, pick_idx, src, w_time, b_time, gain, out,
-    got1a, got1b, out2, got2a, got2b, feats, halo,
+    got1a, got1b, out2, got2a, got2b, feats, halo, total,
     send1, recv1, send2, recv2, send3, recv3,
 ):
     frames = 2
@@ -129,28 +129,43 @@
         def _():
             copy3(f).start()
 
-    for f in range(frames):
-
-        @pl.when(slab > 0)
-        def _():
-            copy3(f).wait_recv()
-
-        @pl.when(slab == 0)
-        def _():
-            halo[f] = jnp.zeros(halo.shape[1:], halo.dtype)
-
     part = group_tiles // 2
+    height = part * 16
+
+    def flat(value):
+        return value.reshape(height, value.shape[-1])
 
     @pl.loop(0, 2)
     def _(c):
         at = pl.ds(c * part, part)
-        seq = [halo[0, at], halo[1, at], feats[0, at], feats[1, at]]
-        seq = [v.reshape(part * 16, v.shape[-1]) for v in seq]
+        own = [flat(feats[0, at]), flat(feats[1, at])]
         for f in range(frames):
-            mixed = seq[2 + f].astype(jnp.float32) + b_time[...]
-            for lag in range(3):
+            mixed = own[f].astype(jnp.float32) + b_time[...]
+            for lag in range(f + 1):
                 mixed = mixed + jnp.dot(
-                    seq[2 + f - lag], w_time[lag], preferred_element_type=jnp.float32
+                    own[f - lag], w_time[lag], preferred_element_type=jnp.float32
+                )
+            total[f, c] = mixed
+
+    for f in range(frames):
+
+        @pl.when(slab > 0)
+        def _():
+            copy3(f).wait_recv()
+
+        @pl.when(slab == 0)
+        def _():
+            halo[f] = jnp.zeros(halo.shape[1:], halo.dtype)
+
+    @pl.loop(0, 2)
+    def _(c):
+        at = pl.ds(c * part, part)
+        before = [flat(halo[0, at]), flat(halo[1, at])]
+        for f in range(frames):
+            mixed = total[f, c]
+            for lag in range(f + 1, 3):
+                mixed = mixed + jnp.dot(
+                    before[2 + f - lag], w_time[lag], preferred_element_type=jnp.float32
                 )
             scale = lax.rsqrt(jnp.mean(mixed * mixed, axis=-1, keepdims=True) + 1e-06)
             value = (mixed * scale * gain[...]).astype(jnp.bfloat16)
@@ -195,6 +210,7 @@
             pltpu.VMEM((rows * bucket, 16, channels), bf16),
             pltpu.VMEM((frames, group_tiles, 16, channels), bf16),
             pltpu.VMEM((frames, group_tiles, 16, channels), bf16),
+            pltpu.VMEM((frames, 2, group_tiles * 8, channels), jnp.float32),
             dma((frames, slabs - 1)),
             dma((frames, slabs - 1)),
             dma((frames, rows - 1)),

time: 77.8 us -> 77.2 us (level)
  no operation moved by 1% of the time
where the time goes in v3:
time: 77.2 us; the launch traced here: 77 us
  Pallas kernels  62.9 us (81%)
  matrix products  6.6 us (9%)
  local copies, waits for them, and re-layouts  5.14 us (7%)
  other arithmetic  2.32 us (3%)
    pallas_call x1, Pallas kernels, body(): pl.pallas_call(functools.partial(kernel, rows, slabs, cap, bucket, group_...  62.9 us
    conv_general_dilated x1, matrix products, conv_space(): lax.conv_general_dilated(grid, w_space, (2, 2), ((1, 1), (1, 1)), dimensi...  6.6 us
    unnamed x3, local copies, waits for them, and re-layouts  2.09 us
    reshape x1, local copies, waits for them, and re-layouts, conv_space(): active.astype(jnp.bfloat16)  2.05 us

profile of v3, /device:TPU:21, one launch (start us, length us, event | category | flops | bytes accessed | tf_op | source)
XLA Modules:
  0.0 77.0 jit_solution(17176763309595155135)
XLA Ops:
  0.0 0.0 copy-start
  0.0 0.9 %reshape.64 = s32[4,48]{1,0:T(4,128)S(1)} reshape(s32[192]{0:T(256)} %param.8) | data formatting | bytes 1536 | tf_op jit(solution)/shard_map/reshape | solution.py:30
  1.0 0.2 convert_reduce_fusion
  1.2 0.1 broadcast_add_fusion
  1.3 0.1 add.51
  1.3 1.4 %select_reduce_fusion.pick_idx = s32[24]{0:T(128)} fusion(s32[192]{0:T(256)S(1)} %add.51, s32[192]{0:T(256)} %param.8, s32[24]{0:T(128)S(1)} %iota_add_fusion), kind=kLoop, calls=%fused_computation.4 | loop fusion | flops 13800 | bytes 1728 | tf_op jit(solution)/shard_map/reduce_sum | solution.py:47
  2.7 0.6 select_reduce_fusion.1.send_idx
  3.3 0.0 copy-done
  3.3 6.6 %multiply_convert_fusion = bf16[96,4,4,512]{3,0,2,1:T(8,128)(2,1)S(1)} fusion(bf16[3,3,256,512]{3,2,1,0:T(8,128)(2,1)S(1)} %copy-done, bf16[96,8,8,256]{3,2,1,0:T(8,128)(2,1)} %bitcast.10, f32[512]{0:T(512)} %param.10), kind=kOutput, calls=%fused_computation.2 | convolution fusion | flops 3049783296 | bytes 7079936 | tf_op jit(solution)/shard_map/conv_general_dilated | solution.py:16
  9.9 2.1 %copy.12.src = bf16[6,16,16,512]{3,2,1,0:T(8,128)(2,1)} copy(bf16[6,16,16,512]{3,1,0,2:T(8,128)(2,1)S(1)} %bitcast.7) | data formatting | bytes 3145728 | tf_op jit(solution)/shard_map/reshape | solution.py:26
  12.0 62.9 %shard_map.73 = bf16[24,2,16,512]{3,2,1,0:T(8,128)(2,1)} custom-call(s32[48]{0:T(128)} %select_reduce_fusion.1.send_idx, s32[24]{0:T(128)} %select_reduce_fusion.pick_idx, bf16[6,16,16,512]{3,2,1,0:T(8,128)(2,1)} %copy.12.src, bf16[3,512,512]{2,1,0:T(8,128)(2,1)} %w_time.1, f32[1,512]{1,0:T(1,128)} %bitcast.8, f32[1,512]{1,0:T(1,128)} %bitcast.9), custom_call_target="tpu_custom_call" | custom-call | tf_op jit(solution)/shard_map/pallas_call | solution.py:200
  74.9 2.1 %copy.18 = bf16[24,2,16,512]{3,2,1,0:T(8,128)(2,1)} copy(bf16[24,2,16,512]{3,2,1,0:T(8,128)(2,1)} %shard_map.73) | data formatting | bytes 1572864
  (5 shorter events, 0.0 us)
Async XLA Ops:
  0.0 3.3 %copy-start = (bf16[3,3,256,512]{3,2,1,0:T(8,128)(2,1)S(1)}, bf16[3,3,256,512]{3,2,1,0:T(8,128)(2,1)}, u32[]{:S(2)}) copy-start(bf16[3,3,256,512]{3,2,1,0:T(8,128)(2,1)} %param.9) | copy-start | bytes 7077892
